TPU v7x, 32 devices: a whole 2x2x4 slice. The times are simulated.
32 devices in a mesh: trow: 4 (over y, x), tcol: 4 (over z), tm: 2 (over core).
Axes of the slice: x: 2, y: 2, z: 4, core: 2. Of those that a mesh axis runs over, the one named last changes fastest.
Arguments:
- start_field: float32 [2, 2, 8, 4096], P('tm', None, None, 'tcol'), may hold values from -6 to 6
- u_tiles: bfloat16 [2, 2, 4096, 2048], P('tm', None, 'trow', 'tcol'), may hold values from -0.25 to 0.25
- v_tiles: bfloat16 [2, 2, 2048, 4096], P('tm', None, 'trow', 'tcol'), may hold values from -0.0546875 to 0.0546875
- rank_blocks: int32 [2, 4, 4], P('tm', 'trow', 'tcol'), may hold values from 1 to 2
- onset_receiver: int32 [8, 4096], P(None, 'trow'), may hold values from 128 to 1023
- onset_source: int32 [8, 4096], P(None, 'tcol'), may hold values from 128 to 1023
- omega: float32 [2], replicated, may hold values from 0.1 to 0.9
Outputs:
- plus_field: float32 [2, 2, 8, 4096], P('tm', None, None, 'tcol')
- minus_field: bfloat16 [2, 2, 8, 4096], P('tm', None, None, 'trow')
Inputs may be any that keep to these rules, and one draw needn't show every extreme that they name: `rank_blocks`: tiles use whole rank blocks; a tile with the most uses all 512 columns.
All inputs are finite; a program needn't handle non-finite values.
Results may differ from a plain program's by a relative error of at most 0.01.
Values may be sent and summed in bfloat16 or wider, within the bound.
A program may use at most 64 MiB of HBM per device.

v0:
```python
import jax
import jax.numpy as jnp
from jax import lax
from jax.sharding import PartitionSpec as P

RBLK = 256
NT = 1024


HIGHEST = lax.Precision.HIGHEST


def window_field(field, onset, omega):
    freq_count = omega.shape[0]
    time_grid = jnp.arange(NT, dtype=jnp.float32)
    time_index = jnp.arange(NT, dtype=jnp.int32)
    phase_grid = omega[:, None] * time_grid[None, :]
    cosine = jnp.cos(phase_grid)
    sine_table = jnp.sin(phase_grid)
    synth_basis = jnp.stack([cosine, -sine_table], axis=1).reshape(2 * freq_count, NT)
    by_point = jnp.transpose(field, (2, 0, 1, 3))

    def per_point(point_pair):
        field_part, limits = point_pair
        coefficients = field_part.reshape(2 * freq_count, field_part.shape[-1])
        traces = jnp.dot(
            coefficients.T, synth_basis, precision=HIGHEST, preferred_element_type=jnp.float32
        )
        keep_mask = time_index[None, :] < limits[:, None]
        traces = jnp.where(keep_mask, traces, jnp.zeros_like(traces))
        real_part = jnp.dot(
            traces, cosine.T, precision=HIGHEST, preferred_element_type=jnp.float32
        ) * (2.0 / NT)
        imag_part = -jnp.dot(
            traces, sine_table.T, precision=HIGHEST, preferred_element_type=jnp.float32
        ) * (2.0 / NT)
        return jnp.stack([real_part.T, imag_part.T], axis=1)

    windowed = lax.map(per_point, (by_point, onset))
    return jnp.transpose(windowed, (1, 2, 0, 3))


def contract_last(left_side, right_side):
    return lax.dot_general(
        left_side, right_side, (((1,), (1,)), ((), ())), preferred_element_type=jnp.float32
    )


def contract_inner(left_side, right_side):
    return lax.dot_general(
        left_side, right_side, (((1,), (0,)), ((), ())), preferred_element_type=jnp.float32
    )


def forward_tile(rows_in, v_part, u_part, live_mask):
    half_rows = rows_in.shape[0] // 2
    first_real = contract_last(rows_in, v_part[0])
    first_imag = contract_last(rows_in, v_part[1])
    t_real = (first_real[:half_rows] - first_imag[half_rows:]) * live_mask
    t_imag = (first_imag[:half_rows] + first_real[half_rows:]) * live_mask
    packed = jnp.concatenate([t_real, t_imag], axis=0).astype(jnp.bfloat16)
    second_real = contract_last(packed, u_part[0])
    second_imag = contract_last(packed, u_part[1])
    return jnp.concatenate(
        [
            second_real[:half_rows] - second_imag[half_rows:],
            second_imag[:half_rows] + second_real[half_rows:],
        ],
        axis=0,
    )


def adjoint_tile(rows_in, u_part, v_part, live_mask):
    half_rows = rows_in.shape[0] // 2
    first_real = contract_inner(rows_in, u_part[0])
    first_imag = contract_inner(rows_in, u_part[1])
    s_real = (first_real[:half_rows] + first_imag[half_rows:]) * live_mask
    s_imag = (first_real[half_rows:] - first_imag[:half_rows]) * live_mask
    packed = jnp.concatenate([s_real, s_imag], axis=0).astype(jnp.bfloat16)
    second_real = contract_inner(packed, v_part[0])
    second_imag = contract_inner(packed, v_part[1])
    return jnp.concatenate(
        [
            second_real[:half_rows] + second_imag[half_rows:],
            second_real[half_rows:] - second_imag[:half_rows],
        ],
        axis=0,
    )


def apply_tile(rows_in, u_tile, v_tile, blocks, adjoint):

    def add_block(block_index, total):
        offset = block_index * RBLK
        u_part = lax.dynamic_slice_in_dim(u_tile, offset, RBLK, 2)
        v_part = lax.dynamic_slice_in_dim(v_tile, offset, RBLK, 1)
        if adjoint:
            return total + adjoint_tile(rows_in, u_part, v_part, 1.0)
        return total + forward_tile(rows_in, v_part, u_part, 1.0)

    start_total = jnp.zeros((rows_in.shape[0], u_tile.shape[1]), jnp.float32)
    return lax.fori_loop(0, blocks, add_block, start_total)


def relay_window(piece, onset_piece, omega, receiver_side):
    spread = lax.all_to_all(piece, "tm", split_axis=3, concat_axis=0, tiled=True)
    windowed = window_field(spread, onset_piece, omega)
    if receiver_side:
        return lax.all_to_all(
            windowed.astype(jnp.bfloat16), "tm", split_axis=0, concat_axis=3, tiled=True
        )
    return lax.all_to_all(windowed, "tm", split_axis=0, concat_axis=3, tiled=True)


def per_device(start_field, u_tiles, v_tiles, rank_blocks, onset_receiver, onset_source, omega):
    u_tile = u_tiles[0]
    v_tile = v_tiles[0]
    blocks = rank_blocks[0, 0, 0]
    points = start_field.shape[2]
    tile_size = u_tile.shape[1]
    col_index = lax.axis_index("tcol")
    row_index = lax.axis_index("trow")
    freq_index = lax.axis_index("tm")
    freq_count = lax.axis_size("tm")
    plus_field = start_field
    rows_in = plus_field.reshape(2 * points, tile_size).astype(jnp.bfloat16)
    partial_value = apply_tile(rows_in, u_tile, v_tile, blocks, False).reshape(
        1, 2, points, tile_size
    )
    piece = lax.psum_scatter(partial_value, "tcol", scatter_dimension=3, tiled=True)
    share_width = piece.shape[3] // freq_count
    onset_piece = lax.dynamic_slice_in_dim(
        onset_receiver, col_index * piece.shape[3] + freq_index * share_width, share_width, 1
    )
    windowed = relay_window(piece, onset_piece, omega, True)
    minus_field = lax.all_gather(windowed, "tcol", axis=3, tiled=True)
    rows_back = minus_field.reshape(2 * points, tile_size)
    partial_back = apply_tile(rows_back, u_tile, v_tile, blocks, True).reshape(
        1, 2, points, tile_size
    )
    piece = lax.psum_scatter(
        partial_back.astype(jnp.bfloat16), "trow", scatter_dimension=3, tiled=True
    ).astype(jnp.float32)
    share_width = piece.shape[3] // freq_count
    onset_piece = lax.dynamic_slice_in_dim(
        onset_source, row_index * piece.shape[3] + freq_index * share_width, share_width, 1
    )
    windowed = relay_window(piece, onset_piece, omega, False)
    source_window = lax.all_gather(windowed, "trow", axis=3, tiled=True)
    plus_field = start_field - source_window
    return (plus_field, minus_field)


def solution(mesh):
    placed = (
        P("tm", None, None, "tcol"),
        P("tm", None, "trow", "tcol"),
        P("tm", None, "trow", "tcol"),
        P("tm", "trow", "tcol"),
        P(None, "trow"),
        P(None, "tcol"),
        P(),
    )
    return jax.shard_map(
        per_device,
        mesh=mesh,
        in_specs=placed,
        out_specs=(P("tm", None, None, "tcol"), P("tm", None, None, "trow")),
        check_vma=False,
    )
```

profile of v0, /device:TPU:0, one launch (start us, length us, event | category | flops | bytes accessed | tf_op | source)
XLA Modules:
  0.0 154.8 jit_solution(5192734265926181508)
XLA Ops:
  7.2 0.8 convert_bitcast_fusion.1
  8.1 6.6 %while.48 = (s32[]{:T(128)}, f32[16,1024]{1,0:T(8,128)S(1)}, s32[]{:T(128)}, bf16[2,512,1024]{2,1,0:T(8,128)(2,1)}, bf16[16,1024]{1,0:T(8,128)(2,1)S(1)}, /*index=5*/bf16[2,1024,512]{2,1,0:T(8,128)(2,1)}) while((s32[]{:T(128)}, f32[16,1024]{1,0:T(8,128)S(1)}, s32[]{:T(128)}, bf16[2,512,1024]{2,1,0:T(8,128)(2,1)}, ...), condition=%wide.region_1.0_spmd.clone, body=%wide.region_0.0_spmd.sunk.clone | while | flops 33644552 | bytes 2777239 | solution.py:102
  8.8 1.3 convolution_bitcast_fusion.12
  10.0 1.3 convolution_bitcast_fusion.13
  11.4 1.3 fusion.121
  12.7 1.3 fusion.120
  15.8 27.3 %reduce-scatter.3.cloned.1.call-done = f32[1,2,8,256]{3,2,1,0:T(8,128)} async-done(((f32[1,2,8,1024]{3,2,1,0:T(8,128)}), f32[1,2,8,256]{3,2,1,0:T(8,128)}) %reduce-scatter.3.cloned.1.call-update) | async-done | bytes 16400 | tf_op jit(solution)/shard_map/reduce_scatter | solution.py:130
  43.1 0.9 copy.23
  44.3 3.7 %all_to_all.72 = f32[2,1,2048]{2,1,0:T(1,128)S(1)} all-to-all(f32[2,1,2048]{2,1,0:T(1,128)S(1)} %reshape.106), channel_id=1, replica_groups=mesh['trow'=4,'tcol'=4,'tm'=2] {'tm'}, dimensions={0} | all-to-all | bytes 32768 | tf_op jit(solution)/shard_map/all_to_all | solution.py:106
  48.6 0.7 reduce
  49.8 16.4 %while.50 = (s32[]{:T(128)}, bf16[8,2,2,128]{3,2,0,1:T(2,128)(2,1)S(1)}, s32[8,128]{1,0:T(8,128)S(1)}, f32[8,2,2,128]{3,0,1,2:T(8,128)S(1)}, f32[4,1024]{1,0:T(4,128)S(1)}, /*index=5*/f32[2]{0:T(128)S(1)}) while((s32[]{:T(128)}, bf16[8,2,2,128]{3,2,0,1:T(2,128)(2,1)S(1)}, s32[8,128]{1,0:T(8,128)S(1)}, ...), condition=%wide.region_4.5_spmd.clone.clone.clone, body=%wide.region_3.4_spmd.clone.clone.sunk.clone | while | flops 12850946 | bytes 1606241 | solution.py:39
  51.2 0.7 fusion.135
  53.2 0.7 fusion.135
  55.3 0.7 fusion.135
  57.3 0.7 fusion.135
  59.4 0.7 fusion.135
  61.4 0.7 fusion.135
  63.5 0.7 fusion.135
  65.6 0.7 fusion.135
  66.3 3.7 %all_to_all.73 = bf16[2,2,8,128]{3,1,2,0:T(2,128)(2,1)S(1)} all-to-all(bf16[2,2,8,128]{3,1,2,0:T(2,128)(2,1)S(1)} %bitcast.232), channel_id=1, replica_groups=mesh['trow'=4,'tcol'=4,'tm'=2] {'tm'}, dimensions={0} | all-to-all | bytes 16384 | tf_op jit(solution)/shard_map/all_to_all | solution.py:109
  70.0 13.1 %all_gather.6 = bf16[1,2,8,1024]{3,2,1,0:T(8,128)(2,1)S(1)} all-gather(bf16[1,2,8,256]{3,2,1,0:T(8,128)(2,1)S(1)} %bitcast.231), channel_id=1, replica_groups=mesh['trow'=4,'tcol'=4,'tm'=2] {'tcol'}, dimensions={3}, use_global_device_ids=true | all-gather | bytes 40960 | tf_op jit(solution)/shard_map/all_gather | solution.py:136
  83.1 4.2 %while.49 = (s32[]{:T(128)}, f32[16,1024]{1,0:T(8,128)S(1)}, s32[]{:T(128)}, bf16[2,1024,512]{2,1,0:T(8,128)(2,1)}, bf16[16,1024]{1,0:T(8,128)(2,1)S(1)}, /*index=5*/bf16[2,512,1024]{2,1,0:T(8,128)(2,1)S(1)}) while((s32[]{:T(128)}, f32[16,1024]{1,0:T(8,128)S(1)}, s32[]{:T(128)}, bf16[2,1024,512]{2,1,0:T(8,128)(2,1)}, ...), condition=%wide.region_6.7_spmd.clone, body=%wide.region_5.6_spmd.sunk.clone | while | flops 33644552 | bytes 2777239 | solution.py:102
  83.8 1.2 convolution_bitcast_fusion.14
  85.0 1.2 convolution_bitcast_fusion.15
  88.0 0.7 constant_dynamic-slice_fusion.5
  88.7 23.6 %reduce-scatter.5.cloned.1.call-done = bf16[1,2,8,256]{3,2,1,0:T(8,128)(2,1)} async-done(((bf16[1,2,8,1024]{3,2,1,0:T(8,128)(2,1)}), bf16[1,2,8,256]{3,2,1,0:T(8,128)(2,1)}) %reduce-scatter.5.cloned.1.call-update) | async-done | bytes 8208 | tf_op jit(solution)/shard_map/reduce_scatter | solution.py:141
  112.3 0.8 copy.28
  113.5 3.7 %all_to_all.74 = f32[2,1,2048]{2,1,0:T(1,128)S(1)} all-to-all(f32[2,1,2048]{2,1,0:T(1,128)S(1)} %reshape.108), channel_id=1, replica_groups=mesh['trow'=4,'tcol'=4,'tm'=2] {'tm'}, dimensions={0} | all-to-all | bytes 32768 | tf_op jit(solution)/shard_map/all_to_all | solution.py:106
  117.2 0.7 reduce.1
  118.5 16.3 %while.51 = (s32[]{:T(128)}, f32[8,2,2,128]{3,2,0,1:T(2,128)S(1)}, s32[8,128]{1,0:T(8,128)S(1)}, f32[8,2,2,128]{3,0,1,2:T(8,128)S(1)}, f32[4,1024]{1,0:T(4,128)S(1)}, /*index=5*/f32[2]{0:T(128)S(1)}) while((s32[]{:T(128)}, f32[8,2,2,128]{3,2,0,1:T(2,128)S(1)}, s32[8,128]{1,0:T(8,128)S(1)}, ...), condition=%wide.region_9.10_spmd.clone.clone.clone, body=%wide.region_8.9_spmd.clone.clone.sunk.clone | while | flops 12850434 | bytes 1611361 | solution.py:39
  134.8 3.7 %all_to_all.75 = f32[2,2,8,128]{3,1,2,0:T(2,128)S(1)} all-to-all(f32[2,2,8,128]{3,1,2,0:T(2,128)S(1)} %bitcast.233), channel_id=1, replica_groups=mesh['trow'=4,'tcol'=4,'tm'=2] {'tm'}, dimensions={0} | all-to-all | bytes 32768 | tf_op jit(solution)/shard_map/all_to_all | solution.py:112
  138.5 8.2 %all_gather.7 = f32[1,2,8,1024]{3,2,1,0:T(8,128)S(1)} all-gather(f32[1,2,8,256]{3,2,1,0:T(8,128)S(1)} %bitcast.228), channel_id=1, replica_groups=mesh['trow'=4,'tcol'=4,'tm'=2] {'trow'}, dimensions={3}, use_global_device_ids=true | all-gather | bytes 81920 | tf_op jit(solution)/shard_map/all_gather | solution.py:149
  (162 shorter events, 32.5 us)
Async XLA Ops:
  7.2 8.6 %copy-start = (s32[8,1024]{1,0:T(8,128)S(1)}, s32[8,1024]{1,0:T(8,128)}, u32[]{:S(2)}) copy-start(s32[8,1024]{1,0:T(8,128)} %param.19) | copy-start | bytes 98308
  7.2 35.9 %reduce-scatter.3.cloned.1.call-start = ((), (), s32[]{:S(2)}) async-start(), calls=%async_computation.6 | async-start | bytes 81920 | tf_op jit(solution)/shard_map/reduce_scatter | solution.py:130
  8.1 7.3 %copy-start.4 = (f32[2]{0:T(128)S(1)}, f32[2]{0:T(128)}, u32[]{:S(2)}) copy-start(f32[2]{0:T(128)} %param.21) | copy-start | bytes 28
  14.7 0.6 copy-start.2
  15.3 97.0 %reduce-scatter.5.cloned.1.call-start = ((), (), s32[]{:S(2)}) async-start(), calls=%async_computation.7 | async-start | bytes 40960 | tf_op jit(solution)/shard_map/reduce_scatter | solution.py:141
  49.3 33.8 %copy-start.1 = (bf16[2,512,1024]{2,1,0:T(8,128)(2,1)S(1)}, bf16[2,512,1024]{2,1,0:T(8,128)(2,1)}, u32[]{:S(2)}) copy-start(bf16[2,512,1024]{2,1,0:T(8,128)(2,1)} %get-tuple-element.644) | copy-start | bytes 6291460
  118.5 28.2 %copy-start.3 = (f32[1,2,8,1024]{3,2,1,0:T(8,128)S(1)}, f32[1,2,8,1024]{3,2,1,0:T(8,128)}, u32[]{:S(2)}) copy-start(f32[1,2,8,1024]{3,2,1,0:T(8,128)} %param.15) | copy-start | bytes 196612
Sparse Core Ops, SparseCore 0:
  15.4 27.6 reduce-scatter.2
  88.1 24.1 reduce-scatter.4
where the time goes:
time: 156 us; the launch traced here: 155 us
  waiting for transfers between devices  50.9 us (33%)
  matrix products  39.1 us (25%)
  blocking collectives  36.2 us (23%)
  between operations  14.2 us (9%)
  local copies, waits for them, and re-layouts  6.64 us (4%)
  other arithmetic  4.16 us (3%)
  loops' own time  3.52 us (2%)
    reduce_scatter x1, waiting for transfers between devices, per_device(): lax.psum_scatter(partial_value, 'tcol', scatter_dimension=3, tiled=True)  27.3 us
    reduce_scatter x1, waiting for transfers between devices, per_device(): lax.psum_scatter(partial_back.astype(jnp.bfloat16), 'trow', scatter_dimen...  23.6 us
    all_gather x1, blocking collectives, per_device(): minus_field = lax.all_gather(windowed, 'tcol', axis=3, tiled=True)  13.1 us
    dot_general x16, matrix products, per_point(): jnp.dot(traces, cosine.T, precision=HIGHEST, preferred_element_type=jnp.f...  10.6 us
    dot_general x16, matrix products, per_point(): jnp.dot(traces, sine_table.T, precision=HIGHEST, preferred_element_type=j...  10.3 us
    dot_general x16, matrix products, per_point(): jnp.dot(coefficients.T, synth_basis, precision=HIGHEST, preferred_element...  10.2 us
    all_gather x1, blocking collectives, per_device(): source_window = lax.all_gather(windowed, 'trow', axis=3, tiled=True)  8.17 us
    all_to_all x2, blocking collectives, relay_window(): lax.all_to_all(piece, 'tm', split_axis=3, concat_axis=0, tiled=True)  7.45 us
  transfers between devices with their start and end apart: 2, of which 2 were waited for; matrix products, arithmetic and copies ran while one was open for 1% of the time, Pallas kernels for 0%

commit v1 on v0

v1 whole, which is shorter than its diff:
```python
import functools

import jax
import jax.numpy as jnp
from jax import lax
from jax.experimental import pallas as pl
from jax.experimental.pallas import tpu as pltpu
from jax.sharding import PartitionSpec as P

RBLK = 256
NT = 1024
MESH = pl.DeviceIdType.MESH
F32 = jnp.float32
BF16 = jnp.bfloat16


def contract_last(left_side, right_side):
    return lax.dot_general(
        left_side, right_side, (((1,), (1,)), ((), ())), preferred_element_type=F32
    )


def contract_inner(left_side, right_side):
    return lax.dot_general(
        left_side, right_side, (((1,), (0,)), ((), ())), preferred_element_type=F32
    )


def sin_cos(angle):
    turns = jnp.floor(angle * 0.6366197723675814 + 0.5)
    rest = angle - turns * 1.5703125
    rest = rest - turns * 4.837512969970703e-4
    rest = rest - turns * 7.549789948768648e-8
    square = rest * rest
    sine = rest + rest * square * (
        -1.6666654611e-1 + square * (8.3321608736e-3 - square * 1.9515295891e-4)
    )
    cosine = 1.0 - 0.5 * square + square * square * (
        4.166664568298827e-2 + square * (-1.388731625493765e-3 + square * 2.443315711809948e-5)
    )
    quarter = turns - 4.0 * jnp.floor(turns * 0.25)
    swap = (quarter == 1.0) | (quarter == 3.0)
    first = jnp.where(swap, cosine, sine)
    second = jnp.where(swap, sine, cosine)
    first = jnp.where(quarter >= 2.0, -first, first)
    second = jnp.where((quarter == 1.0) | (quarter == 2.0), -second, second)
    return first, second


def prefix_sums(phi, count):
    sine, cosine = sin_cos(phi)
    sine_n, cosine_n = sin_cos(count * phi)
    still = phi == 0.0
    ratio = jnp.where(still, count, sine_n / jnp.where(still, 1.0, sine))
    cos_sum = ratio * (cosine_n * cosine + sine_n * sine)
    sin_sum = ratio * (sine_n * cosine - cosine_n * sine)
    return cos_sum, sin_sum


def gram(onset, omega_a, omega_b):
    count = onset.astype(F32)
    omega_a = jnp.full(count.shape, omega_a, F32)
    omega_b = jnp.full(count.shape, omega_b, F32)
    cos_aa, sin_aa = prefix_sums(omega_a, count)
    cos_bb, sin_bb = prefix_sums(omega_b, count)
    cos_sum, sin_sum = prefix_sums(0.5 * (omega_a + omega_b), count)
    cos_dif, sin_dif = prefix_sums(0.5 * (omega_a - omega_b), count)
    scale = 1.0 / NT
    g = {}
    g[0, 0] = scale * (count + cos_aa)
    g[1, 1] = scale * (count - cos_aa)
    g[0, 1] = -scale * sin_aa
    g[2, 2] = scale * (count + cos_bb)
    g[3, 3] = scale * (count - cos_bb)
    g[2, 3] = -scale * sin_bb
    g[0, 2] = scale * (cos_dif + cos_sum)
    g[1, 3] = scale * (cos_dif - cos_sum)
    g[0, 3] = -scale * (sin_sum - sin_dif)
    g[1, 2] = -scale * (sin_sum + sin_dif)
    for m in range(4):
        for n in range(m):
            g[m, n] = g[n, m]
    return g


def apply_gram(g, y):
    return [
        g[m, 0] * y[0] + g[m, 1] * y[1] + g[m, 2] * y[2] + g[m, 3] * y[3] for m in range(4)
    ]


def kernel(
    n_row, n_col, direct_onset,
    start_hbm, u_hbm, v_hbm, rank_ref, onset_r_hbm, onset_s_hbm, omega_ref,
    plus_ref, minus_ref,
    start_buf, u_buf, v_buf, onset_buf, local_sem,
    send1, recv1, send2, recv2, send3, recv3, send4, recv4,
    ssem1, rsem1, ssem2, rsem2, ssem3, rsem3, ssem4, rsem4,
):
    row = lax.axis_index("trow")
    col = lax.axis_index("tcol")
    freq = lax.axis_index("tm")
    group_r, group_s = 2 * n_col, 2 * n_row
    me_r = col * 2 + freq
    me_s = row * 2 + freq
    width_r = recv1.shape[2]
    width_s = recv3.shape[2]

    def peer_r(index):
        return {"tcol": index // 2, "tm": index % 2}

    def peer_s(index):
        return {"trow": index // 2, "tm": index % 2}

    barrier = pltpu.get_barrier_semaphore()
    for step in range(1, group_r):
        pl.semaphore_signal(
            barrier, inc=1, device_id=peer_r((me_r + step) % group_r), device_id_type=MESH
        )
    for step in range(1, group_s):
        pl.semaphore_signal(
            barrier, inc=1, device_id=peer_s((me_s + step) % group_s), device_id_type=MESH
        )

    def onset_src(hbm, me, width):
        if direct_onset:
            return hbm.at[:, pl.ds(pl.multiple_of(me * width, width), width)]
        return hbm.at[me]

    copies = [
        pltpu.make_async_copy(start_hbm.at[0], start_buf, local_sem.at[0]),
        pltpu.make_async_copy(v_hbm.at[0, 0], v_buf.at[0], local_sem.at[1]),
        pltpu.make_async_copy(v_hbm.at[0, 1], v_buf.at[1], local_sem.at[2]),
        pltpu.make_async_copy(u_hbm.at[0, 0], u_buf.at[0], local_sem.at[3]),
        pltpu.make_async_copy(u_hbm.at[0, 1], u_buf.at[1], local_sem.at[4]),
        pltpu.make_async_copy(
            onset_src(onset_r_hbm, me_r, width_r), onset_buf.at[0, :, pl.ds(0, width_r)], local_sem.at[5]
        ),
        pltpu.make_async_copy(
            onset_src(onset_s_hbm, me_s, width_s), onset_buf.at[1, :, pl.ds(0, width_s)], local_sem.at[6]
        ),
    ]
    for copy in copies:
        copy.start()

    def exchange(send_of, recv, ssem, rsem, me, group, peer):
        out = []
        for step in range(1, group):
            index = (me + step) % group
            copy = pltpu.make_async_remote_copy(
                src_ref=send_of(index),
                dst_ref=recv.at[me],
                send_sem=ssem.at[step],
                recv_sem=rsem.at[step],
                device_id=peer(index),
                device_id_type=MESH,
            )
            copy.start()
            out.append(copy)
        return out

    def arrivals(send_of, recv, ssem, rsem, me, group, peer):
        for step in range(1, group):
            index = (me + group - step) % group
            pltpu.make_async_remote_copy(
                src_ref=send_of(index),
                dst_ref=recv.at[index],
                send_sem=ssem.at[step],
                recv_sem=rsem.at[step],
                device_id=peer(index),
                device_id_type=MESH,
            ).wait_recv()

    def window(recv, group, onset, send):
        parts = []
        for k in range(2):
            total = recv[k].astype(F32)
            for other in range(1, group // 2):
                total = total + recv[2 * other + k].astype(F32)
            parts += [total[:8], total[8:]]
        done = apply_gram(onset, parts)
        for k in range(2):
            send[k] = jnp.concatenate([done[2 * k], done[2 * k + 1]], axis=0).astype(BF16)

    def live(width):
        lane = lax.broadcasted_iota(jnp.int32, (8, width), 1)
        return lane < rank_ref[0, 0, 0] * RBLK

    copies[0].wait()
    rows_in = jnp.concatenate([start_buf[0], start_buf[1]], axis=0).astype(BF16)
    copies[1].wait()
    first_real = contract_last(rows_in, v_buf[0])
    copies[2].wait()
    first_imag = contract_last(rows_in, v_buf[1])
    keep = live(first_real.shape[1])
    t_real = jnp.where(keep, first_real[:8] - first_imag[8:], 0.0)
    t_imag = jnp.where(keep, first_imag[:8] + first_real[8:], 0.0)
    packed = jnp.concatenate([t_real, t_imag], axis=0).astype(BF16)
    copies[3].wait()
    second_real = contract_last(packed, u_buf[0])
    copies[4].wait()
    second_imag = contract_last(packed, u_buf[1])
    field = jnp.concatenate(
        [second_real[:8] - second_imag[8:], second_imag[:8] + second_real[8:]], axis=0
    ).astype(BF16)
    for index in range(group_r):
        send1[index] = field[:, index * width_r : (index + 1) * width_r]
    recv1[me_r] = send1[me_r]
    pl.semaphore_wait(barrier, group_r + group_s - 2)

    of1 = lambda index: send1.at[index]
    of2 = lambda index: send2.at[index % 2]
    of3 = lambda index: send3.at[index]
    of4 = lambda index: send4.at[index % 2]
    sent = exchange(of1, recv1, ssem1, rsem1, me_r, group_r, peer_r)

    copies[5].wait()
    copies[6].wait()
    omega_a, omega_b = omega_ref[0], omega_ref[1]
    gram_r = gram(onset_buf[0, :, :width_r], omega_a, omega_b)
    gram_s = gram(onset_buf[1, :, :width_s], omega_a, omega_b)

    arrivals(of1, recv1, ssem1, rsem1, me_r, group_r, peer_r)
    window(recv1, group_r, gram_r, send2)
    sent += exchange(of2, recv2, ssem2, rsem2, me_r, group_r, peer_r)
    recv2[me_r] = send2[freq]
    arrivals(of2, recv2, ssem2, rsem2, me_r, group_r, peer_r)
    rows_back = jnp.concatenate([recv2[index] for index in range(group_r)], axis=1)
    minus_ref[0, 0] = rows_back[:8]
    minus_ref[0, 1] = rows_back[8:]

    first_real = contract_inner(rows_back, u_buf[0])
    first_imag = contract_inner(rows_back, u_buf[1])
    s_real = jnp.where(keep, first_real[:8] + first_imag[8:], 0.0)
    s_imag = jnp.where(keep, first_real[8:] - first_imag[:8], 0.0)
    packed = jnp.concatenate([s_real, s_imag], axis=0).astype(BF16)
    second_real = contract_inner(packed, v_buf[0])
    second_imag = contract_inner(packed, v_buf[1])
    field = jnp.concatenate(
        [second_real[:8] + second_imag[8:], second_real[8:] - second_imag[:8]], axis=0
    ).astype(BF16)
    for index in range(group_s):
        send3[index] = field[:, index * width_s : (index + 1) * width_s]
    recv3[me_s] = send3[me_s]
    sent += exchange(of3, recv3, ssem3, rsem3, me_s, group_s, peer_s)
    arrivals(of3, recv3, ssem3, rsem3, me_s, group_s, peer_s)
    window(recv3, group_s, gram_s, send4)
    sent += exchange(of4, recv4, ssem4, rsem4, me_s, group_s, peer_s)
    recv4[me_s] = send4[freq]
    arrivals(of4, recv4, ssem4, rsem4, me_s, group_s, peer_s)
    back = jnp.concatenate([recv4[index] for index in range(group_s)], axis=1).astype(F32)
    plus_ref[0, 0] = start_buf[0] - back[:8]
    plus_ref[0, 1] = start_buf[1] - back[8:]
    for copy in sent:
        copy.wait_send()


def per_device(start_field, u_tiles, v_tiles, rank_blocks, onset_receiver, onset_source, omega):
    n_row = lax.axis_size("trow")
    n_col = lax.axis_size("tcol")
    group_r, group_s = 2 * n_col, 2 * n_row
    tile_r, tile_s = u_tiles.shape[2], v_tiles.shape[3]
    width_r, width_s = tile_r // group_r, tile_s // group_s
    direct = width_r % 128 == 0 and width_s % 128 == 0
    if not direct:
        onset_receiver = onset_receiver.reshape(8, group_r, width_r).transpose(1, 0, 2)
        onset_source = onset_source.reshape(8, group_s, width_s).transpose(1, 0, 2)
    hbm = pl.BlockSpec(memory_space=pl.ANY)
    smem = pl.BlockSpec(memory_space=pltpu.SMEM)
    vmem = pl.BlockSpec(memory_space=pltpu.VMEM)
    piece_r = lambda count: pltpu.VMEM((count, 16, width_r), BF16)
    piece_s = lambda count: pltpu.VMEM((count, 16, width_s), BF16)
    return pl.pallas_call(
        functools.partial(kernel, n_row, n_col, direct),
        out_shape=(
            jax.ShapeDtypeStruct(start_field.shape, F32),
            jax.ShapeDtypeStruct((1, 2, 8, tile_r), BF16),
        ),
        in_specs=[hbm, hbm, hbm, smem, hbm, hbm, smem],
        out_specs=(vmem, vmem),
        scratch_shapes=[
            pltpu.VMEM(start_field.shape[1:], F32),
            pltpu.VMEM(u_tiles.shape[1:], BF16),
            pltpu.VMEM(v_tiles.shape[1:], BF16),
            pltpu.VMEM((2, 8, max(width_r, width_s)), jnp.int32),
            pltpu.SemaphoreType.DMA((7,)),
            piece_r(group_r), piece_r(group_r), piece_r(2), piece_r(group_r),
            piece_s(group_s), piece_s(group_s), piece_s(2), piece_s(group_s),
        ]
        + [pltpu.SemaphoreType.DMA((group_r,))] * 4
        + [pltpu.SemaphoreType.DMA((group_s,))] * 4,
        compiler_params=pltpu.CompilerParams(
            collective_id=0, has_side_effects=True, vmem_limit_bytes=32 * 1024 * 1024
        ),
    )(start_field, u_tiles, v_tiles, rank_blocks, onset_receiver, onset_source, omega)


def solution(mesh):
    placed = (
        P("tm", None, None, "tcol"),
        P("tm", None, "trow", "tcol"),
        P("tm", None, "trow", "tcol"),
        P("tm", "trow", "tcol"),
        P(None, "trow"),
        P(None, "tcol"),
        P(),
    )
    return jax.shard_map(
        per_device,
        mesh=mesh,
        in_specs=placed,
        out_specs=(P("tm", None, None, "tcol"), P("tm", None, None, "trow")),
        check_vma=False,
    )
```

time: 156 us -> 29.7 us (0.19)
  waiting for transfers between devices: 50.9 us -> 0 us
  matrix products: 39.1 us -> 0 us
  blocking collectives: 36.2 us -> 0 us
  Pallas kernels: 0 us -> 20.6 us
  between operations: 14.2 us -> 1.3 us
  other arithmetic: 4.16 us -> 0 us
  loops' own time: 3.52 us -> 0 us
    reduce_scatter x2 -> x0, waiting for transfers between devices: 50.9 us -> none  [the longest x1 27.3 us: per_device(): lax.psum_scatter(partial_value, 'tcol', scatter_dimension=3, tiled=True)]
    dot_general x56 -> x0, matrix products: 39.1 us -> none  [the longest x16 10.6 us: per_point(): jnp.dot(traces, cosine.T, precision=HIGHEST, preferred_element_type=jnp.f...]
    all_gather x2 -> x0, blocking collectives: 21.3 us -> none  [the longest x1 13.1 us: per_device(): minus_field = lax.all_gather(windowed, 'tcol', axis=3, tiled=True)]
    pallas_call x0 -> x1, Pallas kernels: none -> 20.6 us  [per_device(): pl.pallas_call(functools.partial(kernel, n_row, n_col, direct), out_shape...]
    all_to_all x4 -> x0, blocking collectives: 14.9 us -> none  [the longest x2 7.45 us: relay_window(): lax.all_to_all(piece, 'tm', split_axis=3, concat_axis=0, tiled=True)]
    unnamed x15 -> x14, local copies, waits for them, and re-layouts: 2.87 us -> 7.43 us
    another operation x4 -> x0, loops' own time: 3.52 us -> none  [the longest x2 2.69 us: apply_tile(): return lax.fori_loop(0, blocks, add_block, start_total)]
  transfers between devices with their start and end apart: 2 -> 0, of which waited for: 2 -> 0; matrix products, arithmetic and copies ran while one was open for 1% -> 0% of each run, Pallas kernels for 0% -> 0%
where the time goes in v1:
time: 29.7 us; the launch traced here: 29.3 us
  Pallas kernels  20.6 us (69%)
  local copies, waits for them, and re-layouts  7.43 us (25%)
  between operations  1.3 us (4%)
    pallas_call x1, Pallas kernels, per_device(): pl.pallas_call(functools.partial(kernel, n_row, n_col, direct), out_shape...  20.6 us
    unnamed x14, local copies, waits for them, and re-layouts  7.43 us

profile of v1, /device:TPU:0, one launch (start us, length us, event | category | flops | bytes accessed | tf_op | source)
XLA Modules:
  0.0 29.3 jit_solution(17459145886247133578)
XLA Ops:
  1.3 0.0 copy-start
  1.3 1.6 %copy-done = bf16[1,2,1024,512]{3,2,1,0:T(8,128)(2,1)S(1)} copy-done((bf16[1,2,1024,512]{3,2,1,0:T(8,128)(2,1)S(1)}, bf16[1,2,1024,512]{3,2,1,0:T(8,128)(2,1)}, u32[]{:S(2)}) %copy-start) | copy-done | bytes 2097176
  2.9 0.0 copy-start.1
  2.9 1.6 %copy-done.1 = bf16[1,2,512,1024]{3,2,1,0:T(8,128)(2,1)S(1)} copy-done((bf16[1,2,512,1024]{3,2,1,0:T(8,128)(2,1)S(1)}, bf16[1,2,512,1024]{3,2,1,0:T(8,128)(2,1)}, u32[]{:S(2)}) %copy-start.1) | copy-done | bytes 2097176
  4.5 0.0 copy-start.2
  4.5 0.8 %copy-done.2 = f32[1,2,8,1024]{3,2,1,0:T(8,128)S(1)} copy-done((f32[1,2,8,1024]{3,2,1,0:T(8,128)S(1)}, f32[1,2,8,1024]{3,2,1,0:T(8,128)}, u32[]{:S(2)}) %copy-start.2) | copy-done | bytes 65560
  5.3 0.0 copy-start.3
  5.3 0.8 %copy-done.3 = s32[8,1024]{1,0:T(8,128)S(1)} copy-done((s32[8,1024]{1,0:T(8,128)S(1)}, s32[8,1024]{1,0:T(8,128)}, u32[]{:S(2)}) %copy-start.3) | copy-done | bytes 32792
  6.1 0.0 copy-start.4
  6.1 0.8 %copy-done.4 = s32[8,1024]{1,0:T(8,128)S(1)} copy-done((s32[8,1024]{1,0:T(8,128)S(1)}, s32[8,1024]{1,0:T(8,128)}, u32[]{:S(2)}) %copy-start.4) | copy-done | bytes 32792
  6.8 0.0 copy-start.5
  6.8 0.7 %copy-done.5 = f32[2]{0:T(128)S(1)} copy-done((f32[2]{0:T(128)S(1)}, f32[2]{0:T(128)}, u32[]{:S(2)}) %copy-start.5) | copy-done | bytes 32
  7.5 20.6 %shard_map.86 = (f32[1,2,8,1024]{3,2,1,0:T(8,128)S(1)}, bf16[1,2,8,1024]{3,2,1,0:T(8,128)(2,1)S(1)}) custom-call(f32[1,2,8,1024]{3,2,1,0:T(8,128)S(1)} %copy-done.2, bf16[1,2,1024,512]{3,2,1,0:T(8,128)(2,1)S(1)} %copy-done, bf16[1,2,512,1024]{3,2,1,0:T(8,128)(2,1)S(1)} %copy-done.1, s32[1,1,1]{2,1,0:T(1,128)S(6)} %copy.11.rank_ref, s32[8,1024]{1,0:T(8,128)S(1)} %copy-done.3, ...), custom_call_target="tpu_custom_call" | custom-call | tf_op jit(solution)/shard_map/pallas_call | solution.py:273
  28.1 0.6 %copy.12 = f32[1,2,8,1024]{3,2,1,0:T(8,128)} copy(f32[1,2,8,1024]{3,2,1,0:T(8,128)S(1)} %get-tuple-element.4) | data formatting | bytes 131072
  28.7 0.6 %copy.13 = bf16[1,2,8,1024]{3,2,1,0:T(8,128)(2,1)} copy(bf16[1,2,8,1024]{3,2,1,0:T(8,128)(2,1)S(1)} %get-tuple-element.5) | data formatting | bytes 65536
Async XLA Ops:
  1.3 1.6 %copy-start = (bf16[1,2,1024,512]{3,2,1,0:T(8,128)(2,1)S(1)}, bf16[1,2,1024,512]{3,2,1,0:T(8,128)(2,1)}, u32[]{:S(2)}) copy-start(bf16[1,2,1024,512]{3,2,1,0:T(8,128)(2,1)} %u_hbm.1) | copy-start | bytes 6291460
  2.9 1.6 %copy-start.1 = (bf16[1,2,512,1024]{3,2,1,0:T(8,128)(2,1)S(1)}, bf16[1,2,512,1024]{3,2,1,0:T(8,128)(2,1)}, u32[]{:S(2)}) copy-start(bf16[1,2,512,1024]{3,2,1,0:T(8,128)(2,1)} %v_hbm.1) | copy-start | bytes 6291460
  4.5 0.8 %copy-start.2 = (f32[1,2,8,1024]{3,2,1,0:T(8,128)S(1)}, f32[1,2,8,1024]{3,2,1,0:T(8,128)}, u32[]{:S(2)}) copy-start(f32[1,2,8,1024]{3,2,1,0:T(8,128)} %start_hbm.1) | copy-start | bytes 196612
  5.3 0.8 %copy-start.3 = (s32[8,1024]{1,0:T(8,128)S(1)}, s32[8,1024]{1,0:T(8,128)}, u32[]{:S(2)}) copy-start(s32[8,1024]{1,0:T(8,128)} %onset_r_hbm.1) | copy-start | bytes 98308
  6.1 0.8 %copy-start.4 = (s32[8,1024]{1,0:T(8,128)S(1)}, s32[8,1024]{1,0:T(8,128)}, u32[]{:S(2)}) copy-start(s32[8,1024]{1,0:T(8,128)} %onset_s_hbm.1) | copy-start | bytes 98308
  6.8 0.7 %copy-start.5 = (f32[2]{0:T(128)S(1)}, f32[2]{0:T(128)}, u32[]{:S(2)}) copy-start(f32[2]{0:T(128)} %omega_ref.1) | copy-start | bytes 28

commit v2 on v1

v2 whole, which is shorter than its diff:
```python
import functools

import jax
import jax.numpy as jnp
from jax import lax
from jax.experimental import pallas as pl
from jax.experimental.pallas import tpu as pltpu
from jax.sharding import PartitionSpec as P

RBLK = 256
NT = 1024
MESH = pl.DeviceIdType.MESH
F32 = jnp.float32
BF16 = jnp.bfloat16


def contract_last(left_side, right_side):
    return lax.dot_general(
        left_side, right_side, (((1,), (1,)), ((), ())), preferred_element_type=F32
    )


def contract_inner(left_side, right_side):
    return lax.dot_general(
        left_side, right_side, (((1,), (0,)), ((), ())), preferred_element_type=F32
    )


def sin_cos(angle):
    turns = jnp.floor(angle * 0.6366197723675814 + 0.5)
    rest = angle - turns * 1.5703125
    rest = rest - turns * 4.837512969970703e-4
    rest = rest - turns * 7.549789948768648e-8
    square = rest * rest
    sine = rest + rest * square * (
        -1.6666654611e-1 + square * (8.3321608736e-3 - square * 1.9515295891e-4)
    )
    cosine = 1.0 - 0.5 * square + square * square * (
        4.166664568298827e-2 + square * (-1.388731625493765e-3 + square * 2.443315711809948e-5)
    )
    quarter = turns - 4.0 * jnp.floor(turns * 0.25)
    swap = (quarter == 1.0) | (quarter == 3.0)
    first = jnp.where(swap, cosine, sine)
    second = jnp.where(swap, sine, cosine)
    first = jnp.where(quarter >= 2.0, -first, first)
    second = jnp.where((quarter == 1.0) | (quarter == 2.0), -second, second)
    return first, second


def prefix_sums(phi, count):
    sine, cosine = sin_cos(phi)
    sine_n, cosine_n = sin_cos(count * phi)
    still = phi == 0.0
    ratio = jnp.where(still, count, sine_n / jnp.where(still, 1.0, sine))
    cos_sum = ratio * (cosine_n * cosine + sine_n * sine)
    sin_sum = ratio * (sine_n * cosine - cosine_n * sine)
    return cos_sum, sin_sum


def gram(onset, omega_a, omega_b):
    count = onset.astype(F32)
    omega_a = jnp.full(count.shape, omega_a, F32)
    omega_b = jnp.full(count.shape, omega_b, F32)
    cos_aa, sin_aa = prefix_sums(omega_a, count)
    cos_bb, sin_bb = prefix_sums(omega_b, count)
    cos_sum, sin_sum = prefix_sums(0.5 * (omega_a + omega_b), count)
    cos_dif, sin_dif = prefix_sums(0.5 * (omega_a - omega_b), count)
    scale = 1.0 / NT
    g = {}
    g[0, 0] = scale * (count + cos_aa)
    g[1, 1] = scale * (count - cos_aa)
    g[0, 1] = -scale * sin_aa
    g[2, 2] = scale * (count + cos_bb)
    g[3, 3] = scale * (count - cos_bb)
    g[2, 3] = -scale * sin_bb
    g[0, 2] = scale * (cos_dif + cos_sum)
    g[1, 3] = scale * (cos_dif - cos_sum)
    g[0, 3] = -scale * (sin_sum - sin_dif)
    g[1, 2] = -scale * (sin_sum + sin_dif)
    for m in range(4):
        for n in range(m):
            g[m, n] = g[n, m]
    return g


def apply_gram(g, y):
    return [
        g[m, 0] * y[0] + g[m, 1] * y[1] + g[m, 2] * y[2] + g[m, 3] * y[3] for m in range(4)
    ]


def kernel(
    n_row, n_col, direct_onset,
    start_hbm, u_hbm, v_hbm, rank_ref, onset_r_hbm, onset_s_hbm, omega_hbm,
    out_ref,
    start_buf, u_buf, v_buf, omega_ref, onset_r_buf, onset_s_buf, local_sem,
    send1, recv1, send2, recv2, send3, recv3, send4, recv4,
    ssem1, rsem1, ssem2, rsem2, ssem3, rsem3, ssem4, rsem4,
):
    row = lax.axis_index("trow")
    col = lax.axis_index("tcol")
    freq = lax.axis_index("tm")
    group_r, group_s = 2 * n_col, 2 * n_row
    me_r = col * 2 + freq
    me_s = row * 2 + freq
    width_r = recv1.shape[2]
    half_s = recv3.shape[2]
    half_r = u_buf.shape[1] // 2
    half_group = group_r // 2

    def peer_r(index):
        return {"tcol": index // 2, "tm": index % 2}

    def peer_s(index):
        return {"trow": index // 2, "tm": index % 2}

    far = 1 - me_r // half_group
    near = 1 - far
    far_rows = pl.ds(pl.multiple_of(far * half_r, half_r), half_r)
    near_rows = pl.ds(pl.multiple_of(near * half_r, half_r), half_r)
    if direct_onset:
        onset_r_src = onset_r_hbm.at[:, pl.ds(pl.multiple_of(me_r * width_r, width_r), width_r)]
    else:
        onset_r_src = onset_r_hbm.at[me_r]
    onset_s_src = onset_s_hbm.at[:, pl.ds(pl.multiple_of(freq * half_s, half_s), half_s)]
    moves = [
        (start_hbm.at[0], start_buf),
        (v_hbm.at[0, 0], v_buf.at[0]),
        (v_hbm.at[0, 1], v_buf.at[1]),
        (u_hbm.at[0, 0, far_rows], u_buf.at[0, far_rows]),
        (u_hbm.at[0, 1, far_rows], u_buf.at[1, far_rows]),
        (u_hbm.at[0, 0, near_rows], u_buf.at[0, near_rows]),
        (u_hbm.at[0, 1, near_rows], u_buf.at[1, near_rows]),
        (omega_hbm, omega_ref),
        (onset_r_src, onset_r_buf),
        (onset_s_src, onset_s_buf),
    ]
    copies = [
        pltpu.make_async_copy(source, target, local_sem.at[place])
        for place, (source, target) in enumerate(moves)
    ]
    for copy in copies:
        copy.start()

    barrier = pltpu.get_barrier_semaphore()
    for step in range(1, group_r):
        pl.semaphore_signal(
            barrier, inc=1, device_id=peer_r((me_r + step) % group_r), device_id_type=MESH
        )
    for step in range(1, group_s):
        pl.semaphore_signal(
            barrier, inc=1, device_id=peer_s((me_s + step) % group_s), device_id_type=MESH
        )

    def remote(source, target, ssem, rsem, device):
        return pltpu.make_async_remote_copy(
            src_ref=source, dst_ref=target, send_sem=ssem, recv_sem=rsem,
            device_id=device, device_id_type=MESH,
        )

    sent = []

    def push(send_of, recv, ssem, rsem, me, index, peer):
        copy = remote(send_of(index), recv.at[me], ssem.at[index], rsem.at[me], peer(index))
        copy.start()
        sent.append(copy)

    def arrivals(send_of, recv, ssem, rsem, me, group, peer):
        for step in range(1, group):
            index = (me + step) % group
            remote(
                send_of(index), recv.at[index], ssem.at[index], rsem.at[index], peer(index)
            ).wait_recv()

    def window(recv, group, onset):
        parts = []
        for k in range(2):
            total = recv[k].astype(F32)
            for other in range(1, group // 2):
                total = total + recv[2 * other + k].astype(F32)
            parts += [total[:8], total[8:]]
        done = apply_gram(onset, parts)
        return [
            jnp.concatenate([done[2 * k], done[2 * k + 1]], axis=0).astype(BF16)
            for k in range(2)
        ]

    of1 = lambda index: send1.at[index]
    of2 = lambda index: send2.at[index % 2]
    of3 = lambda index: send3.at[index % 2]

    copies[0].wait()
    rows_in = jnp.concatenate([start_buf[0], start_buf[1]], axis=0).astype(BF16)
    copies[1].wait()
    first_real = contract_last(rows_in, v_buf[0])
    copies[2].wait()
    first_imag = contract_last(rows_in, v_buf[1])
    lane = lax.broadcasted_iota(jnp.int32, (8, first_real.shape[1]), 1)
    keep = lane < rank_ref[0, 0, 0] * RBLK
    t_real = jnp.where(keep, first_real[:8] - first_imag[8:], 0.0)
    t_imag = jnp.where(keep, first_imag[:8] + first_real[8:], 0.0)
    packed = jnp.concatenate([t_real, t_imag], axis=0).astype(BF16)

    def forward_half(half, rows, real_copy, imag_copy):
        real_copy.wait()
        second_real = contract_last(packed, u_buf[0, rows])
        imag_copy.wait()
        second_imag = contract_last(packed, u_buf[1, rows])
        field = jnp.concatenate(
            [second_real[:8] - second_imag[8:], second_imag[:8] + second_real[8:]], axis=0
        ).astype(BF16)
        for place in range(half_group):
            send1[half * half_group + place] = field[:, place * width_r : (place + 1) * width_r]

    forward_half(far, far_rows, copies[3], copies[4])
    pl.semaphore_wait(barrier, group_r + group_s - 2)
    for place in range(half_group):
        push(of1, recv1, ssem1, rsem1, me_r, far * half_group + place, peer_r)
    forward_half(near, near_rows, copies[5], copies[6])
    for step in range(1, half_group):
        push(
            of1, recv1, ssem1, rsem1, me_r,
            near * half_group + (me_r + step) % half_group, peer_r,
        )
    recv1[me_r] = send1[me_r]
    for place in (7, 8, 9):
        copies[place].wait()
    gram_r = gram(onset_r_buf[...], omega_ref[0], omega_ref[1])

    arrivals(of1, recv1, ssem1, rsem1, me_r, group_r, peer_r)
    done = window(recv1, group_r, gram_r)
    for k in range(2):
        send2[k] = done[k]
    for step in range(1, group_r):
        push(of2, recv2, ssem2, rsem2, me_r, (me_r + step) % group_r, peer_r)
    recv2[me_r] = send2[freq]
    gram_s = gram(onset_s_buf[...], omega_ref[0], omega_ref[1])
    arrivals(of2, recv2, ssem2, rsem2, me_r, group_r, peer_r)
    rows_back = jnp.concatenate([recv2[index] for index in range(group_r)], axis=1)

    first_real = contract_inner(rows_back, u_buf[0])
    first_imag = contract_inner(rows_back, u_buf[1])
    s_real = jnp.where(keep, first_real[:8] + first_imag[8:], 0.0)
    s_imag = jnp.where(keep, first_real[8:] - first_imag[:8], 0.0)
    packed_back = jnp.concatenate([s_real, s_imag], axis=0).astype(BF16)
    for half in range(2):
        span = slice(half * half_s, (half + 1) * half_s)
        second_real = contract_inner(packed_back, v_buf[0, :, span])
        second_imag = contract_inner(packed_back, v_buf[1, :, span])
        send3[half] = jnp.concatenate(
            [second_real[:8] + second_imag[8:], second_real[8:] - second_imag[:8]], axis=0
        ).astype(BF16)
        for step in range(1, n_row):
            push(
                of3, recv3, ssem3, rsem3, me_s, ((row + step) % n_row) * 2 + half, peer_s
            )
    partner = me_s + 1 - 2 * freq
    push(of3, recv3, ssem3, rsem3, me_s, partner, peer_s)
    recv3[me_s] = send3[freq]
    out_ref[1, 0] = rows_back[:8]
    out_ref[1, 1] = rows_back[8:]
    arrivals(of3, recv3, ssem3, rsem3, me_s, group_s, peer_s)
    done = window(recv3, group_s, gram_s)
    for k in range(2):
        send4[k] = done[k]
    last = remote(send4.at[1 - freq], recv4.at[freq], ssem4, rsem4, {"tm": 1 - freq})
    last.start()
    recv4[freq] = send4[freq]
    remote(send4.at[freq], recv4.at[1 - freq], ssem4, rsem4, {"tm": 1 - freq}).wait_recv()
    back = jnp.concatenate([recv4[0], recv4[1]], axis=1)
    out_ref[0, 0] = back[:8]
    out_ref[0, 1] = back[8:]
    for copy in sent:
        copy.wait_send()
    last.wait_send()


def per_device(start_field, u_tiles, v_tiles, rank_blocks, onset_receiver, onset_source, omega):
    n_row = lax.axis_size("trow")
    n_col = lax.axis_size("tcol")
    group_r, group_s = 2 * n_col, 2 * n_row
    tile_r, tile_s = u_tiles.shape[2], v_tiles.shape[3]
    width_r, half_s = tile_r // group_r, tile_s // 2
    direct = width_r % 128 == 0
    if not direct:
        onset_receiver = onset_receiver.reshape(8, group_r, width_r).transpose(1, 0, 2)
    hbm = pl.BlockSpec(memory_space=pl.ANY)
    piece_r = lambda count: pltpu.VMEM((count, 16, width_r), BF16)
    piece_s = lambda count: pltpu.VMEM((count, 16, half_s), BF16)
    sems = pltpu.SemaphoreType.DMA
    fields = pl.pallas_call(
        functools.partial(kernel, n_row, n_col, direct),
        out_shape=jax.ShapeDtypeStruct((2, 2, 8, tile_r), BF16),
        in_specs=[hbm] * 3 + [pl.BlockSpec(memory_space=pltpu.SMEM)] + [hbm] * 3,
        out_specs=pl.BlockSpec(memory_space=pltpu.VMEM),
        scratch_shapes=[
            pltpu.VMEM(start_field.shape[1:], F32),
            pltpu.VMEM(u_tiles.shape[1:], BF16),
            pltpu.VMEM(v_tiles.shape[1:], BF16),
            pltpu.SMEM((2,), F32),
            pltpu.VMEM((8, width_r), jnp.int32),
            pltpu.VMEM((8, half_s), jnp.int32),
            sems((10,)),
            piece_r(group_r), piece_r(group_r), piece_r(2), piece_r(group_r),
            piece_s(2), piece_s(group_s), piece_s(2), piece_s(2),
        ]
        + [sems((group_r,))] * 4
        + [sems((group_s,))] * 2
        + [sems(())] * 2,
        compiler_params=pltpu.CompilerParams(
            collective_id=0, has_side_effects=True, vmem_limit_bytes=24 * 1024 * 1024
        ),
    )(
        pin(start_field), pin(u_tiles), pin(v_tiles), rank_blocks,
        pin(onset_receiver), pin(onset_source), pin(omega),
    )
    return start_field - fields[:1].astype(F32), fields[1:]


def pin(x):
    return pltpu.with_memory_space_constraint(x, pltpu.MemorySpace.HBM)


def solution(mesh):
    placed = (
        P("tm", None, None, "tcol"),
        P("tm", None, "trow", "tcol"),
        P("tm", None, "trow", "tcol"),
        P("tm", "trow", "tcol"),
        P(None, "trow"),
        P(None, "tcol"),
        P(),
    )
    return jax.shard_map(
        per_device,
        mesh=mesh,
        in_specs=placed,
        out_specs=(P("tm", None, None, "tcol"), P("tm", None, None, "trow")),
        check_vma=False,
    )
```

time: 29.7 us -> 21.4 us (0.72)
  local copies, waits for them, and re-layouts: 7.43 us -> 0.62 us
  Pallas kernels: 20.6 us -> 18.6 us
  other arithmetic: 0 us -> 0.64 us
    unnamed x14 -> x2, local copies, waits for them, and re-layouts: 7.43 us -> 0.01 us
    pallas_call x1, Pallas kernels: 20.6 us -> 18.6 us  [per_device(): pl.pallas_call(functools.partial(kernel, n_row, n_col, direct), out_shape...]
    sub x0 -> x1, other arithmetic: none -> 0.64 us  [per_device(): return (start_field - fields[:1].astype(F32), fields[1:])]
    slice x0 -> x1, local copies, waits for them, and re-layouts: none -> 0.62 us  [per_device(): return (start_field - fields[:1].astype(F32), fields[1:])]
where the time goes in v2:
time: 21.4 us; the launch traced here: 21.2 us
  Pallas kernels  18.6 us (87%)
  between operations  1.29 us (6%)
  other arithmetic  0.64 us (3%)
  local copies, waits for them, and re-layouts  0.62 us (3%)
    pallas_call x1, Pallas kernels, per_device(): pl.pallas_call(functools.partial(kernel, n_row, n_col, direct), out_shape...  18.6 us
    sub x1, other arithmetic, per_device(): return (start_field - fields[:1].astype(F32), fields[1:])  0.64 us
    slice x1, local copies, waits for them, and re-layouts, per_device(): return (start_field - fields[:1].astype(F32), fields[1:])  0.62 us

profile of v2, /device:TPU:0, one launch (start us, length us, event | category | flops | bytes accessed | tf_op | source)
XLA Modules:
  0.0 21.2 jit_solution(17161638218168572672)
XLA Ops:
  1.3 0.0 copy-start
  1.3 18.6 %shard_map.86 = bf16[2,2,8,1024]{3,2,1,0:T(8,128)(2,1)S(1)} custom-call(f32[1,2,8,1024]{3,2,1,0:T(8,128)} %start_hbm.1, bf16[1,2,1024,512]{3,2,1,0:T(8,128)(2,1)} %u_hbm.1, bf16[1,2,512,1024]{3,2,1,0:T(8,128)(2,1)} %v_hbm.1, s32[1,1,1]{2,1,0:T(1,128)S(6)} %copy.9.rank_ref, s32[8,1024]{1,0:T(8,128)} %onset_r_hbm.1, s32[8,1024]{1,0:T(8,128)} %onset_s_hbm.1, ...), custom_call_target="tpu_custom_call" | custom-call | tf_op jit(solution)/shard_map/pallas_call | solution.py:291
  19.9 0.6 %slice.7 = bf16[1,2,8,1024]{3,2,1,0:T(8,128)(2,1)} slice(bf16[2,2,8,1024]{3,2,1,0:T(8,128)(2,1)S(1)} %shard_map.86), slice={[1:2], [0:2], [0:8], [0:1024]} | slice | bytes 65536 | tf_op jit(solution)/shard_map/slice | solution.py:317
  20.6 0.0 copy-done
  20.6 0.6 %convert_subtract_fusion = f32[1,2,8,1024]{3,2,1,0:T(8,128)} fusion(f32[1,2,8,1024]{3,2,1,0:T(8,128)S(1)} %copy-done, bf16[2,2,8,1024]{3,2,1,0:T(8,128)(2,1)S(1)} %shard_map.86), kind=kLoop, calls=%fused_computation | loop fusion | flops 32768 | bytes 163840 | tf_op jit(solution)/shard_map/sub | solution.py:317
Async XLA Ops:
  1.3 19.3 %copy-start = (f32[1,2,8,1024]{3,2,1,0:T(8,128)S(1)}, f32[1,2,8,1024]{3,2,1,0:T(8,128)}, u32[]{:S(2)}) copy-start(f32[1,2,8,1024]{3,2,1,0:T(8,128)} %start_hbm.1) | copy-start | bytes 196612

commit v3 on v2

--- a/solution.py
+++ b/solution.py
@@ -90,7 +90,7 @@
 
 
 def kernel(
-    n_row, n_col, direct_onset,
+    n_row, n_col,
     start_hbm, u_hbm, v_hbm, rank_ref, onset_r_hbm, onset_s_hbm, omega_hbm,
     out_ref,
     start_buf, u_buf, v_buf, omega_ref, onset_r_buf, onset_s_buf, local_sem,
@@ -103,10 +103,8 @@
     group_r, group_s = 2 * n_col, 2 * n_row
     me_r = col * 2 + freq
     me_s = row * 2 + freq
-    width_r = recv1.shape[2]
     half_s = recv3.shape[2]
     half_r = u_buf.shape[1] // 2
-    half_group = group_r // 2
 
     def peer_r(index):
         return {"tcol": index // 2, "tm": index % 2}
@@ -114,23 +112,16 @@
     def peer_s(index):
         return {"trow": index // 2, "tm": index % 2}
 
-    far = 1 - me_r // half_group
-    near = 1 - far
-    far_rows = pl.ds(pl.multiple_of(far * half_r, half_r), half_r)
-    near_rows = pl.ds(pl.multiple_of(near * half_r, half_r), half_r)
-    if direct_onset:
-        onset_r_src = onset_r_hbm.at[:, pl.ds(pl.multiple_of(me_r * width_r, width_r), width_r)]
-    else:
-        onset_r_src = onset_r_hbm.at[me_r]
+    onset_r_src = onset_r_hbm.at[:, pl.ds(pl.multiple_of(freq * half_r, half_r), half_r)]
     onset_s_src = onset_s_hbm.at[:, pl.ds(pl.multiple_of(freq * half_s, half_s), half_s)]
     moves = [
         (start_hbm.at[0], start_buf),
         (v_hbm.at[0, 0], v_buf.at[0]),
         (v_hbm.at[0, 1], v_buf.at[1]),
-        (u_hbm.at[0, 0, far_rows], u_buf.at[0, far_rows]),
-        (u_hbm.at[0, 1, far_rows], u_buf.at[1, far_rows]),
-        (u_hbm.at[0, 0, near_rows], u_buf.at[0, near_rows]),
-        (u_hbm.at[0, 1, near_rows], u_buf.at[1, near_rows]),
+        (u_hbm.at[0, 0, pl.ds(0, half_r)], u_buf.at[0, pl.ds(0, half_r)]),
+        (u_hbm.at[0, 1, pl.ds(0, half_r)], u_buf.at[1, pl.ds(0, half_r)]),
+        (u_hbm.at[0, 0, pl.ds(half_r, half_r)], u_buf.at[0, pl.ds(half_r, half_r)]),
+        (u_hbm.at[0, 1, pl.ds(half_r, half_r)], u_buf.at[1, pl.ds(half_r, half_r)]),
         (omega_hbm, omega_ref),
         (onset_r_src, onset_r_buf),
         (onset_s_src, onset_s_buf),
@@ -185,8 +176,7 @@
             for k in range(2)
         ]
 
-    of1 = lambda index: send1.at[index]
-    of2 = lambda index: send2.at[index % 2]
+    of1 = lambda index: send1.at[index % 2]
     of3 = lambda index: send3.at[index % 2]
 
     copies[0].wait()
@@ -201,28 +191,23 @@
     t_imag = jnp.where(keep, first_imag[:8] + first_real[8:], 0.0)
     packed = jnp.concatenate([t_real, t_imag], axis=0).astype(BF16)
 
-    def forward_half(half, rows, real_copy, imag_copy):
-        real_copy.wait()
+    for half in range(2):
+        rows = pl.ds(half * half_r, half_r)
+        copies[3 + 2 * half].wait()
         second_real = contract_last(packed, u_buf[0, rows])
-        imag_copy.wait()
+        copies[4 + 2 * half].wait()
         second_imag = contract_last(packed, u_buf[1, rows])
-        field = jnp.concatenate(
+        send1[half] = jnp.concatenate(
             [second_real[:8] - second_imag[8:], second_imag[:8] + second_real[8:]], axis=0
         ).astype(BF16)
-        for place in range(half_group):
-            send1[half * half_group + place] = field[:, place * width_r : (place + 1) * width_r]
-
-    forward_half(far, far_rows, copies[3], copies[4])
-    pl.semaphore_wait(barrier, group_r + group_s - 2)
-    for place in range(half_group):
-        push(of1, recv1, ssem1, rsem1, me_r, far * half_group + place, peer_r)
-    forward_half(near, near_rows, copies[5], copies[6])
-    for step in range(1, half_group):
-        push(
-            of1, recv1, ssem1, rsem1, me_r,
-            near * half_group + (me_r + step) % half_group, peer_r,
-        )
-    recv1[me_r] = send1[me_r]
+        if half == 0:
+            pl.semaphore_wait(barrier, group_r + group_s - 2)
+        for step in range(1, n_col):
+            push(
+                of1, recv1, ssem1, rsem1, me_r, ((col + step) % n_col) * 2 + half, peer_r
+            )
+    push(of1, recv1, ssem1, rsem1, me_r, me_r + 1 - 2 * freq, peer_r)
+    recv1[me_r] = send1[freq]
     for place in (7, 8, 9):
         copies[place].wait()
     gram_r = gram(onset_r_buf[...], omega_ref[0], omega_ref[1])
@@ -231,12 +216,12 @@
     done = window(recv1, group_r, gram_r)
     for k in range(2):
         send2[k] = done[k]
-    for step in range(1, group_r):
-        push(of2, recv2, ssem2, rsem2, me_r, (me_r + step) % group_r, peer_r)
-    recv2[me_r] = send2[freq]
+    middle = remote(send2.at[1 - freq], recv2.at[freq], ssem2, rsem2, {"tm": 1 - freq})
+    middle.start()
+    recv2[freq] = send2[freq]
     gram_s = gram(onset_s_buf[...], omega_ref[0], omega_ref[1])
-    arrivals(of2, recv2, ssem2, rsem2, me_r, group_r, peer_r)
-    rows_back = jnp.concatenate([recv2[index] for index in range(group_r)], axis=1)
+    remote(send2.at[freq], recv2.at[1 - freq], ssem2, rsem2, {"tm": 1 - freq}).wait_recv()
+    rows_back = jnp.concatenate([recv2[0], recv2[1]], axis=1)
 
     first_real = contract_inner(rows_back, u_buf[0])
     first_imag = contract_inner(rows_back, u_buf[1])
@@ -272,6 +257,7 @@
     out_ref[0, 1] = back[8:]
     for copy in sent:
         copy.wait_send()
+    middle.wait_send()
     last.wait_send()
 
 
@@ -280,16 +266,13 @@
     n_col = lax.axis_size("tcol")
     group_r, group_s = 2 * n_col, 2 * n_row
     tile_r, tile_s = u_tiles.shape[2], v_tiles.shape[3]
-    width_r, half_s = tile_r // group_r, tile_s // 2
-    direct = width_r % 128 == 0
-    if not direct:
-        onset_receiver = onset_receiver.reshape(8, group_r, width_r).transpose(1, 0, 2)
+    half_r, half_s = tile_r // 2, tile_s // 2
     hbm = pl.BlockSpec(memory_space=pl.ANY)
-    piece_r = lambda count: pltpu.VMEM((count, 16, width_r), BF16)
+    piece_r = lambda count: pltpu.VMEM((count, 16, half_r), BF16)
     piece_s = lambda count: pltpu.VMEM((count, 16, half_s), BF16)
     sems = pltpu.SemaphoreType.DMA
     fields = pl.pallas_call(
-        functools.partial(kernel, n_row, n_col, direct),
+        functools.partial(kernel, n_row, n_col),
         out_shape=jax.ShapeDtypeStruct((2, 2, 8, tile_r), BF16),
         in_specs=[hbm] * 3 + [pl.BlockSpec(memory_space=pltpu.SMEM)] + [hbm] * 3,
         out_specs=pl.BlockSpec(memory_space=pltpu.VMEM),
@@ -298,13 +281,14 @@
             pltpu.VMEM(u_tiles.shape[1:], BF16),
             pltpu.VMEM(v_tiles.shape[1:], BF16),
             pltpu.SMEM((2,), F32),
-            pltpu.VMEM((8, width_r), jnp.int32),
+            pltpu.VMEM((8, half_r), jnp.int32),
             pltpu.VMEM((8, half_s), jnp.int32),
             sems((10,)),
-            piece_r(group_r), piece_r(group_r), piece_r(2), piece_r(group_r),
+            piece_r(2), piece_r(group_r), piece_r(2), piece_r(2),
             piece_s(2), piece_s(group_s), piece_s(2), piece_s(2),
         ]
-        + [sems((group_r,))] * 4
+        + [sems((group_r,))] * 2
+        + [sems(())] * 2
         + [sems((group_s,))] * 2
         + [sems(())] * 2,
         compiler_params=pltpu.CompilerParams(

time: 21.4 us -> 19.5 us (0.911)
  Pallas kernels: 18.6 us -> 16.8 us
    pallas_call x1, Pallas kernels: 18.6 us -> 16.8 us  [per_device(): pl.pallas_call(functools.partial(kernel, n_row, n_col), out_shape=jax.Sha...]
where the time goes in v3:
time: 19.5 us; the launch traced here: 19.4 us
  Pallas kernels  16.8 us (86%)
  between operations  1.29 us (7%)
  other arithmetic  0.64 us (3%)
  local copies, waits for them, and re-layouts  0.62 us (3%)
    pallas_call x1, Pallas kernels, per_device(): pl.pallas_call(functools.partial(kernel, n_row, n_col), out_shape=jax.Sha...  16.8 us
    sub x1, other arithmetic, per_device(): return (start_field - fields[:1].astype(F32), fields[1:])  0.64 us
    slice x1, local copies, waits for them, and re-layouts, per_device(): return (start_field - fields[:1].astype(F32), fields[1:])  0.62 us

profile of v3, /device:TPU:0, one launch (start us, length us, event | category | flops | bytes accessed | tf_op | source)
XLA Modules:
  0.0 19.4 jit_solution(17911072372088890739)
XLA Ops:
  1.3 0.0 copy-start
  1.3 16.8 %shard_map.86 = bf16[2,2,8,1024]{3,2,1,0:T(8,128)(2,1)S(1)} custom-call(f32[1,2,8,1024]{3,2,1,0:T(8,128)} %start_hbm.1, bf16[1,2,1024,512]{3,2,1,0:T(8,128)(2,1)} %u_hbm.1, bf16[1,2,512,1024]{3,2,1,0:T(8,128)(2,1)} %v_hbm.1, s32[1,1,1]{2,1,0:T(1,128)S(6)} %copy.9.rank_ref, s32[8,1024]{1,0:T(8,128)} %onset_r_hbm.1, s32[8,1024]{1,0:T(8,128)} %onset_s_hbm.1, ...), custom_call_target="tpu_custom_call" | custom-call | tf_op jit(solution)/shard_map/pallas_call | solution.py:274
  18.1 0.6 %slice.7 = bf16[1,2,8,1024]{3,2,1,0:T(8,128)(2,1)} slice(bf16[2,2,8,1024]{3,2,1,0:T(8,128)(2,1)S(1)} %shard_map.86), slice={[1:2], [0:2], [0:8], [0:1024]} | slice | bytes 65536 | tf_op jit(solution)/shard_map/slice | solution.py:301
  18.7 0.0 copy-done
  18.7 0.6 %convert_subtract_fusion = f32[1,2,8,1024]{3,2,1,0:T(8,128)} fusion(f32[1,2,8,1024]{3,2,1,0:T(8,128)S(1)} %copy-done, bf16[2,2,8,1024]{3,2,1,0:T(8,128)(2,1)S(1)} %shard_map.86), kind=kLoop, calls=%fused_computation | loop fusion | flops 32768 | bytes 163840 | tf_op jit(solution)/shard_map/sub | solution.py:301
Async XLA Ops:
  1.3 17.5 %copy-start = (f32[1,2,8,1024]{3,2,1,0:T(8,128)S(1)}, f32[1,2,8,1024]{3,2,1,0:T(8,128)}, u32[]{:S(2)}) copy-start(f32[1,2,8,1024]{3,2,1,0:T(8,128)} %start_hbm.1) | copy-start | bytes 196612

commit v4 on v3

--- a/solution.py
+++ b/solution.py
@@ -220,11 +220,17 @@
     middle.start()
     recv2[freq] = send2[freq]
     gram_s = gram(onset_s_buf[...], omega_ref[0], omega_ref[1])
+    own_rows = pl.ds(pl.multiple_of(freq * half_r, half_r), half_r)
+    other_rows = pl.ds(pl.multiple_of((1 - freq) * half_r, half_r), half_r)
+    own = send2[freq]
+    own_real = contract_inner(own, u_buf[0, own_rows])
+    own_imag = contract_inner(own, u_buf[1, own_rows])
     remote(send2.at[freq], recv2.at[1 - freq], ssem2, rsem2, {"tm": 1 - freq}).wait_recv()
     rows_back = jnp.concatenate([recv2[0], recv2[1]], axis=1)
 
-    first_real = contract_inner(rows_back, u_buf[0])
-    first_imag = contract_inner(rows_back, u_buf[1])
+    other = recv2[1 - freq]
+    first_real = own_real + contract_inner(other, u_buf[0, other_rows])
+    first_imag = own_imag + contract_inner(other, u_buf[1, other_rows])
     s_real = jnp.where(keep, first_real[:8] + first_imag[8:], 0.0)
     s_imag = jnp.where(keep, first_real[8:] - first_imag[:8], 0.0)
     packed_back = jnp.concatenate([s_real, s_imag], axis=0).astype(BF16)

time: 19.5 us -> 19.5 us (level)
  no operation moved by 1% of the time
where the time goes in v4:
time: 19.5 us; the launch traced here: 19.4 us
  Pallas kernels  16.8 us (86%)
  between operations  1.29 us (7%)
  other arithmetic  0.64 us (3%)
  local copies, waits for them, and re-layouts  0.62 us (3%)
    pallas_call x1, Pallas kernels, per_device(): pl.pallas_call(functools.partial(kernel, n_row, n_col), out_shape=jax.Sha...  16.8 us
    sub x1, other arithmetic, per_device(): return (start_field - fields[:1].astype(F32), fields[1:])  0.64 us
    slice x1, local copies, waits for them, and re-layouts, per_device(): return (start_field - fields[:1].astype(F32), fields[1:])  0.62 us

profile of v4, /device:TPU:0, one launch (start us, length us, event | category | flops | bytes accessed | tf_op | source)
XLA Modules:
  0.0 19.4 jit_solution(3753284475589303653)
XLA Ops:
  1.3 0.0 copy-start
  1.3 16.8 %shard_map.86 = bf16[2,2,8,1024]{3,2,1,0:T(8,128)(2,1)S(1)} custom-call(f32[1,2,8,1024]{3,2,1,0:T(8,128)} %start_hbm.1, bf16[1,2,1024,512]{3,2,1,0:T(8,128)(2,1)} %u_hbm.1, bf16[1,2,512,1024]{3,2,1,0:T(8,128)(2,1)} %v_hbm.1, s32[1,1,1]{2,1,0:T(1,128)S(6)} %copy.9.rank_ref, s32[8,1024]{1,0:T(8,128)} %onset_r_hbm.1, s32[8,1024]{1,0:T(8,128)} %onset_s_hbm.1, ...), custom_call_target="tpu_custom_call" | custom-call | tf_op jit(solution)/shard_map/pallas_call | solution.py:280
  18.1 0.6 %slice.7 = bf16[1,2,8,1024]{3,2,1,0:T(8,128)(2,1)} slice(bf16[2,2,8,1024]{3,2,1,0:T(8,128)(2,1)S(1)} %shard_map.86), slice={[1:2], [0:2], [0:8], [0:1024]} | slice | bytes 65536 | tf_op jit(solution)/shard_map/slice | solution.py:307
  18.7 0.0 copy-done
  18.7 0.6 %convert_subtract_fusion = f32[1,2,8,1024]{3,2,1,0:T(8,128)} fusion(f32[1,2,8,1024]{3,2,1,0:T(8,128)S(1)} %copy-done, bf16[2,2,8,1024]{3,2,1,0:T(8,128)(2,1)S(1)} %shard_map.86), kind=kLoop, calls=%fused_computation | loop fusion | flops 32768 | bytes 163840 | tf_op jit(solution)/shard_map/sub | solution.py:307
Async XLA Ops:
  1.3 17.5 %copy-start = (f32[1,2,8,1024]{3,2,1,0:T(8,128)S(1)}, f32[1,2,8,1024]{3,2,1,0:T(8,128)}, u32[]{:S(2)}) copy-start(f32[1,2,8,1024]{3,2,1,0:T(8,128)} %start_hbm.1) | copy-start | bytes 196612
